TPU v7x, 32 devices: a whole 2x2x4 slice. The times are simulated.
32 devices in a mesh: dp: 4 (over z), mp: 8 (over y, x, core).
Axes of the slice: x: 2, y: 2, z: 4, core: 2. Of those that a mesh axis runs over, the one named last changes fastest.
Arguments:
- block_input: bfloat16 [8192, 2048], P(('dp', 'mp')), may hold values from -6 to 6
- out_cotangent: bfloat16 [8192, 2048], P(('dp', 'mp')), may hold values from -6 to 6
- objective: int32 [16], P('dp'), may hold values from 0 to 1, as said below
- prefix_len: int32 [16], P('dp'), may hold values from 64 to 511
- target_mask: int32 [8192], P(('dp', 'mp')), may hold values from 0 to 1, as said below
- qkv_weight: float32 [2048, 3, 2048], P('dp', None, 'mp'), may hold values from -0.125 to 0.125
- out_weight: float32 [2048, 2048], P('mp', 'dp'), may hold values from -3 to 3
- gateup_weight: float32 [2048, 2, 5472], P('dp', None, 'mp'), may hold values from -0.125 to 0.125
- down_weight: float32 [5472, 2048], P('mp', 'dp'), may hold values from -0.625 to 0.625
- norm_params: float32 [4, 2048], replicated, as said below
- qkv_first: float32 [2048, 3, 2048], P('dp', None, 'mp'), may hold values from -0.125 to 0.125
- out_first: float32 [2048, 2048], P('mp', 'dp'), may hold values from -0.005859375 to 0.005859375
- gateup_first: float32 [2048, 2, 5472], P('dp', None, 'mp'), may hold values from -0.09375 to 0.09375
- down_first: float32 [5472, 2048], P('mp', 'dp'), may hold values from -0.013671875 to 0.013671875
- norm_first: float32 [4, 2048], replicated, may hold values from -0.21875 to 0.21875
- qkv_second: float32 [2048, 3, 2048], P('dp', None, 'mp'), may hold values from 3.0517578e-05 to 0.00048828125
- out_second: float32 [2048, 2048], P('mp', 'dp'), may hold values from 7.080078e-08 to 1.1230469e-06
- gateup_second: float32 [2048, 2, 5472], P('dp', None, 'mp'), may hold values from 1.953125e-05 to 0.0003125
- down_second: float32 [5472, 2048], P('mp', 'dp'), may hold values from 4.3945312e-07 to 7.080078e-06
- norm_second: float32 [4, 2048], replicated, may hold values from 0.00012207031 to 0.001953125
Outputs:
- block_output: bfloat16 [8192, 2048], P(('dp', 'mp'))
- input_grad: float32 [8192, 2048], P(('dp', 'mp'))
- qkv_new: float32 [2048, 3, 2048], P('dp', None, 'mp')
- qkv_first_new: float32 [2048, 3, 2048], P('dp', None, 'mp')
- qkv_second_new: float32 [2048, 3, 2048], P('dp', None, 'mp')
- out_new: float32 [2048, 2048], P('mp', 'dp')
- out_first_new: float32 [2048, 2048], P('mp', 'dp')
- out_second_new: float32 [2048, 2048], P('mp', 'dp')
- gateup_new: float32 [2048, 2, 5472], P('dp', None, 'mp')
- gateup_first_new: float32 [2048, 2, 5472], P('dp', None, 'mp')
- gateup_second_new: float32 [2048, 2, 5472], P('dp', None, 'mp')
- down_new: float32 [5472, 2048], P('mp', 'dp')
- down_first_new: float32 [5472, 2048], P('mp', 'dp')
- down_second_new: float32 [5472, 2048], P('mp', 'dp')
- norm_new: float32 [4, 2048], replicated
- norm_first_new: float32 [4, 2048], replicated
- norm_second_new: float32 [4, 2048], replicated
Inputs may be any that keep to these rules, and one draw needn't show every extreme that they name: `objective`: at least one sequence of each kind. `target_mask`: the last residue of every sequence is a target. `norm_params`: rows 0 and 2 are the gains of the first and second norm, rows 1 and 3 their biases.
All inputs are finite; a program needn't handle non-finite values.
Results may differ from a plain program's by a relative error of at most 0.024.
Values may be sent and summed in bfloat16 or wider, within the bound.
No kernel may reach another device: no remote copies, remote signals or barrier semaphores. Data moves between devices by JAX's collectives and lax.ppermute only.
A program may use at most 256 MiB of HBM per device.

v0:
```python
import jax
import jax.numpy as jnp
from jax import lax
from jax.sharding import PartitionSpec as P

D = 2048
HD = 128
FF = 5461
FF_PAD = 5472
STEP = 5
deep_alpha = 48.0**0.5
norm_eps = 1e-05
masked_score = -1e30
rope_base = 10000.0
beta_one = 0.5
beta_two = 0.5
adam_eps = 1e-08
decay_rate = 0.1


def rope_tables(seq_len, head_dim):
    position = jnp.arange(seq_len, dtype=jnp.float32)
    freqs = rope_base ** (-jnp.arange(0, head_dim, 2, dtype=jnp.float32) / head_dim)
    angles = position[:, None] * freqs[None, :]
    return (jnp.cos(angles), jnp.sin(angles))


def rotate(values, cosine, sine_table):
    half_dim = values.shape[-1] // 2
    first_half = values[..., :half_dim]
    second_half = values[..., half_dim:]
    cos_b = cosine[:, None, :]
    sin_b = sine_table[:, None, :]
    return jnp.concatenate(
        [first_half * cos_b - second_half * sin_b, second_half * cos_b + first_half * sin_b], -1
    )


def norm_forward(hidden, norm_gain, norm_bias):
    row_mean = jnp.mean(hidden, -1, keepdims=True)
    centred = hidden - row_mean
    variance = jnp.mean(centred * centred, -1, keepdims=True)
    inv_std = lax.rsqrt(variance + norm_eps)
    normed = centred * inv_std
    return (normed * norm_gain + norm_bias, normed, inv_std)


def norm_backward(grad_rows, normed, inv_std, norm_gain):
    grad_normed = grad_rows * norm_gain
    mean_grad = jnp.mean(grad_normed, -1, keepdims=True)
    mean_proj = jnp.mean(grad_normed * normed, -1, keepdims=True)
    grad_in = inv_std * (grad_normed - mean_grad - normed * mean_proj)
    return (grad_in, jnp.sum(grad_rows * normed, 0), jnp.sum(grad_rows, 0))


def adamw(weight, gradient, first_moment, second, step_rate):
    first_new = beta_one * first_moment + (1.0 - beta_one) * gradient
    second_new = beta_two * second + (1.0 - beta_two) * gradient * gradient
    first_hat = first_new / (1.0 - beta_one**STEP)
    second_hat = second_new / (1.0 - beta_two**STEP)
    weight_new = weight - step_rate * (
        first_hat / (jnp.sqrt(second_hat) + adam_eps) + decay_rate * weight
    )
    return (weight_new, first_new, second_new)


def local(
    block_input,
    out_cotangent,
    objective,
    prefix_len,
    target_mask,
    qkv_weight,
    out_weight,
    gateup_weight,
    down_weight,
    norm_params,
    qkv_first,
    out_first,
    gateup_first,
    down_first,
    norm_first,
    qkv_second,
    out_second,
    gateup_second,
    down_second,
    norm_second,
):
    mp_count = lax.axis_size("mp")
    mp_index = lax.axis_index("mp")
    own_rows = block_input.shape[0]
    seq_count = objective.shape[0]
    group_rows = own_rows * mp_count
    seq_len = group_rows // seq_count
    local_dim = qkv_weight.shape[2]
    local_heads = local_dim // HD
    local_units = gateup_weight.shape[2]
    score_scale = HD ** (-0.5)
    row_start = mp_index * own_rows
    qkv_full, out_full, gateup_full, down_full = (
        lax.all_gather(qkv_weight.astype(jnp.bfloat16), "dp", axis=0, tiled=True),
        lax.all_gather(out_weight.astype(jnp.bfloat16), "dp", axis=1, tiled=True),
        lax.all_gather(gateup_weight.astype(jnp.bfloat16), "dp", axis=0, tiled=True),
        lax.all_gather(down_weight.astype(jnp.bfloat16), "dp", axis=1, tiled=True),
    )
    input_all = lax.all_gather(block_input, "mp", axis=0, tiled=True)
    projected = jnp.einsum("td,dce->tce", input_all, qkv_full, preferred_element_type=jnp.float32)
    shaped = projected.reshape(seq_count, seq_len, 3, local_heads, HD)
    cosine, sine_table = rope_tables(seq_len, HD)
    query_rows = rotate(shaped[:, :, 0], cosine, sine_table).astype(jnp.bfloat16)
    key_rows = rotate(shaped[:, :, 1], cosine, sine_table).astype(jnp.bfloat16)
    value_rows = shaped[:, :, 2].astype(jnp.bfloat16)
    row_index = jnp.arange(seq_len)[:, None]
    col_index = jnp.arange(seq_len)[None, :]
    visible = (
        (objective[:, None, None] > 0)
        | (col_index[None] < prefix_len[:, None, None])
        | (col_index <= row_index)[None]
    )
    scores = (
        jnp.einsum("sihe,sjhe->shij", query_rows, key_rows, preferred_element_type=jnp.float32)
        * score_scale
    )
    scores = jnp.where(visible[:, None], scores, masked_score)
    row_max = jnp.max(scores, -1, keepdims=True)
    exp_scores = jnp.exp(scores - row_max)
    row_total = jnp.sum(exp_scores, -1, keepdims=True)
    soft_weights = exp_scores / row_total
    log_total = row_max + jnp.log(row_total)
    attended = jnp.einsum(
        "shij,sjhe->sihe",
        soft_weights.astype(jnp.bfloat16),
        value_rows,
        preferred_element_type=jnp.float32,
    )
    attended_low = attended.reshape(group_rows, local_dim).astype(jnp.bfloat16)
    attn_part = jnp.dot(attended_low, out_full, preferred_element_type=jnp.float32)
    attn_total = lax.psum(attn_part, "mp")
    hidden_all = deep_alpha * input_all.astype(jnp.float32) + attn_total
    middle_all, _, _ = norm_forward(hidden_all, norm_params[0], norm_params[1])
    middle_low = middle_all.astype(jnp.bfloat16)
    hidden_one = lax.dynamic_slice_in_dim(hidden_all, row_start, own_rows, 0)
    middle = lax.dynamic_slice_in_dim(middle_all, row_start, own_rows, 0)
    live_units = (mp_index * local_units + jnp.arange(local_units) < FF).astype(jnp.float32)
    gate_up = jnp.einsum("td,dcf->tcf", middle_low, gateup_full, preferred_element_type=jnp.float32)
    hidden_low = (jax.nn.gelu(gate_up[:, 0]) * gate_up[:, 1] * live_units).astype(jnp.bfloat16)
    ffn_part = jnp.dot(hidden_low, down_full, preferred_element_type=jnp.float32)
    ffn_total = lax.psum(ffn_part.astype(jnp.bfloat16), "mp").astype(jnp.float32)
    ffn_own = lax.dynamic_slice_in_dim(ffn_total, row_start, own_rows, 0)
    hidden_two = deep_alpha * middle + ffn_own
    output_rows, normed_two, inv_two = norm_forward(hidden_two, norm_params[2], norm_params[3])
    mask_f32 = target_mask.astype(jnp.float32)
    grad_rows = out_cotangent.astype(jnp.float32) * mask_f32[:, None]
    grad_two, gain_two, bias_two = norm_backward(grad_rows, normed_two, inv_two, norm_params[2])
    ffn_back = lax.all_gather(grad_two.astype(jnp.bfloat16), "mp", axis=0, tiled=True)
    gate_again = jnp.einsum(
        "td,dcf->tcf", middle_low, gateup_full, preferred_element_type=jnp.float32
    )
    gate_act, gelu_pull = jax.vjp(jax.nn.gelu, gate_again[:, 0])
    up_part = gate_again[:, 1]
    hidden_again = (gate_act * up_part * live_units).astype(jnp.bfloat16)
    grad_hidden = (
        jnp.einsum("td,fd->tf", ffn_back, down_full, preferred_element_type=jnp.float32)
        * live_units
    )
    down_grad = jnp.einsum("tf,td->fd", hidden_again, ffn_back, preferred_element_type=jnp.float32)
    grad_gate = gelu_pull(grad_hidden * up_part)[0]
    grad_up = grad_hidden * gate_act
    grad_gateup = jnp.stack([grad_gate, grad_up], 1).astype(jnp.bfloat16)
    middle_part = jnp.einsum(
        "tcf,dcf->td", grad_gateup, gateup_full, preferred_element_type=jnp.float32
    )
    gateup_grad = jnp.einsum(
        "td,tcf->dcf", middle_low, grad_gateup, preferred_element_type=jnp.float32
    )
    grad_middle = (
        lax.psum_scatter(
            middle_part.astype(jnp.bfloat16), "mp", scatter_dimension=0, tiled=True
        ).astype(jnp.float32)
        + deep_alpha * grad_two
    )
    _, normed_one, inv_one = norm_forward(hidden_one, norm_params[0], norm_params[1])
    grad_one, gain_one, bias_one = norm_backward(grad_middle, normed_one, inv_one, norm_params[0])
    attn_back = lax.all_gather(grad_one.astype(jnp.bfloat16), "mp", axis=0, tiled=True)
    grad_attended = jnp.einsum(
        "td,ed->te", attn_back, out_full, preferred_element_type=jnp.float32
    ).astype(jnp.bfloat16)
    grad_attended = grad_attended.reshape(seq_count, seq_len, local_heads, HD)
    out_grad = jnp.einsum("te,td->ed", attended_low, attn_back, preferred_element_type=jnp.float32)
    scores_again = (
        jnp.einsum("sihe,sjhe->shij", query_rows, key_rows, preferred_element_type=jnp.float32)
        * score_scale
    )
    scores_again = jnp.where(visible[:, None], scores_again, masked_score)
    soft_again = jnp.exp(scores_again - log_total)
    grad_soft = jnp.einsum(
        "sihe,sjhe->shij", grad_attended, value_rows, preferred_element_type=jnp.float32
    )
    value_grad = jnp.einsum(
        "shij,sihe->sjhe",
        soft_again.astype(jnp.bfloat16),
        grad_attended,
        preferred_element_type=jnp.float32,
    )
    row_dot = jnp.sum(soft_again * grad_soft, -1, keepdims=True)
    grad_scores = (soft_again * (grad_soft - row_dot)).astype(jnp.bfloat16)
    query_grad = (
        jnp.einsum("shij,sjhe->sihe", grad_scores, key_rows, preferred_element_type=jnp.float32)
        * score_scale
    )
    key_grad = (
        jnp.einsum("shij,sihe->sjhe", grad_scores, query_rows, preferred_element_type=jnp.float32)
        * score_scale
    )
    query_lin = rotate(query_grad, cosine, -sine_table)
    key_lin = rotate(key_grad, cosine, -sine_table)
    grad_proj = (
        jnp.stack([query_lin, key_lin, value_grad], 2)
        .astype(jnp.bfloat16)
        .reshape(group_rows, 3, local_dim)
    )
    input_part = jnp.einsum("tce,dce->td", grad_proj, qkv_full, preferred_element_type=jnp.float32)
    qkv_grad = jnp.einsum("td,tce->dce", input_all, grad_proj, preferred_element_type=jnp.float32)
    input_raw = (
        lax.psum_scatter(
            input_part.astype(jnp.bfloat16), "mp", scatter_dimension=0, tiled=True
        ).astype(jnp.float32)
        + deep_alpha * grad_one
    )
    qkv_grad, out_grad, gateup_grad, down_grad = (
        lax.psum_scatter(
            qkv_grad.astype(jnp.bfloat16), "dp", scatter_dimension=0, tiled=True
        ).astype(jnp.float32),
        lax.psum_scatter(
            out_grad.astype(jnp.bfloat16), "dp", scatter_dimension=1, tiled=True
        ).astype(jnp.float32),
        lax.psum_scatter(
            gateup_grad.astype(jnp.bfloat16), "dp", scatter_dimension=0, tiled=True
        ).astype(jnp.float32),
        lax.psum_scatter(
            down_grad.astype(jnp.bfloat16), "dp", scatter_dimension=1, tiled=True
        ).astype(jnp.float32),
    )
    norm_grad = jnp.stack([gain_one, bias_one, gain_two, bias_two], 0)
    norm_grad, target_count = lax.psum((norm_grad, jnp.sum(mask_f32)), ("dp", "mp"))
    rate_list = (D ** (-0.5), 0.5, D ** (-0.5), (FF_PAD // 64) ** (-0.5), 0.4)
    qkv_res = adamw(qkv_weight, qkv_grad / target_count, qkv_first, qkv_second, rate_list[0])
    out_res = adamw(out_weight, out_grad / target_count, out_first, out_second, rate_list[1])
    gateup_res = adamw(
        gateup_weight, gateup_grad / target_count, gateup_first, gateup_second, rate_list[2]
    )
    down_res = adamw(down_weight, down_grad / target_count, down_first, down_second, rate_list[3])
    norm_res = adamw(norm_params, norm_grad / target_count, norm_first, norm_second, rate_list[4])
    return (
        output_rows.astype(jnp.bfloat16),
        input_raw / target_count,
        qkv_res[0],
        qkv_res[1],
        qkv_res[2],
        out_res[0],
        out_res[1],
        out_res[2],
        gateup_res[0],
        gateup_res[1],
        gateup_res[2],
        down_res[0],
        down_res[1],
        down_res[2],
        norm_res[0],
        norm_res[1],
        norm_res[2],
    )


def solution(mesh):
    return jax.shard_map(
        local,
        mesh=mesh,
        in_specs=(
            P(("dp", "mp"), None),
            P(("dp", "mp"), None),
            P("dp"),
            P("dp"),
            P(("dp", "mp")),
            P("dp", None, "mp"),
            P("mp", "dp"),
            P("dp", None, "mp"),
            P("mp", "dp"),
            P(),
            P("dp", None, "mp"),
            P("mp", "dp"),
            P("dp", None, "mp"),
            P("mp", "dp"),
            P(),
            P("dp", None, "mp"),
            P("mp", "dp"),
            P("dp", None, "mp"),
            P("mp", "dp"),
            P(),
        ),
        out_specs=(
            P(("dp", "mp"), None),
            P(("dp", "mp"), None),
            P("dp", None, "mp"),
            P("dp", None, "mp"),
            P("dp", None, "mp"),
            P("mp", "dp"),
            P("mp", "dp"),
            P("mp", "dp"),
            P("dp", None, "mp"),
            P("dp", None, "mp"),
            P("dp", None, "mp"),
            P("mp", "dp"),
            P("mp", "dp"),
            P("mp", "dp"),
            P(),
            P(),
            P(),
        ),
        check_vma=False,
    )
```

profile of v0, /device:TPU:0, one launch (start us, length us, event | category | flops | bytes accessed | tf_op | source)
XLA Modules:
  0.0 1279.1 jit_solution(2433256142239264889)
XLA Ops:
  14.7 61.7 %all-gather.10.cloned.1.call-done = bf16[2048,3,256]{2,0,1:T(8,128)(2,1)} async-done(((bf16[512,3,256]{2,0,1:T(8,128)(2,1)}), bf16[2048,3,256]{2,0,1:T(8,128)(2,1)}) %all-gather.10.cloned.1.call-update) | async-done | bytes 3145744 | tf_op jit(solution)/shard_map/all_gather | solution.py:101
  76.4 54.8 %all-gather.8.cloned.1.call-done = bf16[2048,2048]{1,0:T(8,128)(2,1)} async-done(((bf16[256,2048]{1,0:T(8,128)(2,1)}), bf16[2048,2048]{1,0:T(8,128)(2,1)}) %all-gather.8.cloned.1.call-update) | async-done | bytes 8388624 | tf_op jit(solution)/shard_map/all_gather | solution.py:106
  131.2 11.6 fusion.6
  142.8 8.3 reshape.239
  173.4 11.4 copy.105
  184.8 9.7 fusion.51
  200.8 211.6 %all-reduce.4.cloned.1.call-done = f32[2048,2048]{1,0:T(8,128)} async-done(((f32[2048,2048]{1,0:T(8,128)}), f32[2048,2048]{1,0:T(8,128)}) %all-reduce.4.cloned.1.call-update) | async-done | bytes 16777232 | tf_op jit(solution)/shard_map/psum | solution.py:138
  412.5 16.0 %fusion.81 = (f32[2048]{0:T(1024)S(1)}, f32[2048,2048]{1,0:T(8,128)}) fusion(f32[2048,2048]{1,0:T(8,128)} %all-reduce.4.cloned.1.call-done, bf16[2048,2048]{1,0:T(8,128)(2,1)} %all-gather.8.cloned.1.call-done), kind=kLoop, calls=%fused_computation.166 | loop fusion | flops 16775168 | bytes 41951232 | tf_op jit(solution)/shard_map/reduce_sum | solution.py:40
  428.5 7.7 multiply_reduce_fusion
  436.2 12.2 multiply_add_fusion
  448.5 69.6 %all-gather.14.cloned.1.call-done = bf16[2048,2,684]{0,1,2:T(2,128)(2,1)} async-done(((bf16[512,2,684]{0,1,2:T(2,128)(2,1)}), bf16[2048,2,684]{0,1,2:T(2,128)(2,1)}) %all-gather.14.cloned.1.call-update) | async-done | bytes 5603344 | tf_op jit(solution)/shard_map/all_gather | solution.py:103
  518.1 22.3 %fusion.2 = f32[2048,2,684]{0,2,1:T(8,128)} fusion(bf16[2048,2,684]{0,1,2:T(2,128)(2,1)} %all-gather.14.cloned.1.call-done, f32[2048,2048]{1,0:T(8,128)} %multiply_add_fusion), kind=kOutput, calls=%fused_computation.7 | convolution fusion | flops 11479810048 | bytes 33587200 | tf_op jit(solution)/shard_map/td,dcf->tcf/dot_general | solution.py:145
  545.8 30.5 %all-gather.16.cloned.1.call-done = bf16[684,2048]{1,0:T(8,128)(2,1)} async-done(((bf16[684,512]{1,0:T(8,128)(2,1)}), bf16[684,2048]{1,0:T(8,128)(2,1)}) %all-gather.16.cloned.1.call-update) | async-done | bytes 2801680 | tf_op jit(solution)/shard_map/all_gather | solution.py:104
  576.3 11.2 convolution_convert_fusion
  588.2 124.4 %all-reduce.6.cloned.1.call-done = bf16[2048,2048]{1,0:T(8,128)(2,1)} async-done(((bf16[2048,2048]{1,0:T(8,128)(2,1)}), bf16[2048,2048]{1,0:T(8,128)(2,1)}) %all-reduce.6.cloned.1.call-update) | async-done | bytes 8388624 | tf_op jit(solution)/shard_map/psum | solution.py:148
  719.2 54.5 %all-gather.18.cloned.1.call-done = bf16[2048,2048]{1,0:T(8,128)(2,1)} async-done(((bf16[256,2048]{1,0:T(8,128)(2,1)}), bf16[2048,2048]{1,0:T(8,128)(2,1)}) %all-gather.18.cloned.1.call-update) | async-done | bytes 8388624 | tf_op jit(solution)/shard_map/all_gather | solution.py:155
  773.7 15.4 %fusion.36 = (bf16[2048,1,684]{0,2,1:T(8,128)(2,1)S(1)}, bf16[2048,1,684]{0,2,1:T(8,128)(2,1)S(1)}) fusion(f32[2048,2,684]{0,2,1:T(8,128)} %fusion.2, f32[684]{0:T(1024)S(1)} %fusion.66, bf16[2048,2048]{1,0:T(8,128)(2,1)} %all-gather.18.cloned.1.call-done, bf16[684,2048]{1,0:T(8,128)(2,1)} %all-gather.16.cloned.1.call-done), kind=kOutput, calls=%fused_computation.56 | convolution fusion | flops 5772828672 | bytes 28002992 | tf_op jit(solution)/shard_map/td,fd->tf/dot_general | solution.py:163
  791.6 17.9 %bitcast_convert_fusion.1 = bf16[2048,2048]{1,0:T(8,128)(2,1)} fusion(bf16[2048,2,684]{0,1,2:T(2,128)(2,1)} %all-gather.14.cloned.1.call-done, bf16[2048,1,684]{0,2,1:T(8,128)(2,1)S(1)} %get-tuple-element.102, bf16[2048,1,684]{0,2,1:T(8,128)(2,1)S(1)} %get-tuple-element.101), kind=kOutput, calls=%fused_computation.1 | convolution fusion | flops 11482611712 | bytes 19595264 | tf_op jit(solution)/shard_map/tcf,dcf->td/dot_general | solution.py:170
  813.5 67.7 %reduce-scatter.7.cloned.1.call-done = bf16[256,2048]{1,0:T(8,128)(2,1)} async-done(((bf16[2048,2048]{1,0:T(8,128)(2,1)}), bf16[256,2048]{1,0:T(8,128)(2,1)}) %reduce-scatter.7.cloned.1.call-update) | async-done | bytes 1048592 | tf_op jit(solution)/shard_map/reduce_scatter | solution.py:177
  888.4 18.6 %fusion.19 = bf16[2048,2,684]{0,2,1:T(8,128)(2,1)} fusion(f32[2048,2048]{1,0:T(8,128)} %multiply_add_fusion, bf16[2048,1,684]{0,2,1:T(8,128)(2,1)} %copy-done.49, bf16[2048,1,684]{0,2,1:T(8,128)(2,1)} %copy-done.48), kind=kOutput, calls=%fused_computation.39 | convolution fusion | flops 11493818368 | bytes 27983872 | tf_op jit(solution)/shard_map/td,tcf->dcf/dot_general | solution.py:173
  908.8 10.6 convolution_convert_fusion.1
  920.2 22.6 %all-gather.20.cloned.1.call-done = bf16[2048,2048]{1,0:T(8,128)(2,1)} async-done(((bf16[256,2048]{1,0:T(8,128)(2,1)}), bf16[2048,2048]{1,0:T(8,128)(2,1)}) %all-gather.20.cloned.1.call-update) | async-done | bytes 8388624 | tf_op jit(solution)/shard_map/all_gather | solution.py:184
  942.7 5.8 convolution_convert_fusion.3
  949.6 6.0 fusion.46
  984.3 6.8 convolution_convert_fusion.2
  993.3 12.0 fusion.31
  1007.1 10.8 bitcast_convert_fusion
  1027.8 41.6 %all-reduce = (f32[]{:T(128)}, f32[4,2048]{1,0:T(4,128)S(1)}) all-reduce(f32[]{:T(128)} %convert_reduce_fusion, f32[4,2048]{1,0:T(4,128)S(1)} %pad_maximum_fusion.11), channel_id=1, replica_groups=mesh['dp'=4,'mp'=8] {'dp','mp'}, use_global_device_ids=true, to_apply=%region_18.19 | all-reduce | flops 8193 | bytes 65544 | tf_op jit(solution)/shard_map/psum | solution.py:245
  1087.2 16.2 %reduce-scatter.17.cloned.1.call-done = bf16[684,512]{1,0:T(8,128)(2,1)} async-done(((bf16[684,2048]{1,0:T(8,128)(2,1)}), bf16[684,512]{1,0:T(8,128)(2,1)}) %reduce-scatter.17.cloned.1.call-update) | async-done | bytes 700432 | tf_op jit(solution)/shard_map/reduce_scatter | solution.py:240
  1108.6 24.2 %reduce-scatter.13.cloned.1.call-done = bf16[256,512]{1,0:T(8,128)(2,1)} async-done(((bf16[256,2048]{1,0:T(8,128)(2,1)}), bf16[256,512]{1,0:T(8,128)(2,1)}) %reduce-scatter.13.cloned.1.call-update) | async-done | bytes 262160 | tf_op jit(solution)/shard_map/reduce_scatter | solution.py:234
  1136.4 57.5 %reduce-scatter.11.cloned.1.call-done = bf16[512,3,256]{0,2,1:T(8,128)(2,1)} async-done(((bf16[2048,3,256]{0,2,1:T(8,128)(2,1)}), bf16[512,3,256]{0,2,1:T(8,128)(2,1)}) %reduce-scatter.11.cloned.1.call-update) | async-done | bytes 786448 | tf_op jit(solution)/shard_map/reduce_scatter | solution.py:231
  1208.9 59.7 %reduce-scatter.9.cloned.1.call-done = bf16[256,2048]{1,0:T(8,128)(2,1)} async-done(((bf16[2048,2048]{1,0:T(8,128)(2,1)}), bf16[256,2048]{1,0:T(8,128)(2,1)}) %reduce-scatter.9.cloned.1.call-update) | async-done | bytes 1048592 | tf_op jit(solution)/shard_map/reduce_scatter | solution.py:225
  (208 shorter events, 153.3 us)
Async XLA Ops:
  7.2 6.0 copy-start.47
  7.2 6.0 copy-start.46
  7.2 69.1 %all-gather.10.cloned.1.call-start = ((), (), s32[]{:S(2)}) async-start(), calls=%async_computation.7 | async-start | bytes 3932160 | tf_op jit(solution)/shard_map/all_gather | solution.py:101
  9.7 121.5 %all-gather.8.cloned.1.call-start = ((), (), s32[]{:S(2)}) async-start(), calls=%async_computation.6 | async-start | bytes 9437184 | tf_op jit(solution)/shard_map/all_gather | solution.py:106
  10.5 174.4 %all-gather.12.cloned.1.call-start = ((), (), s32[]{:S(2)}) async-start(), calls=%async_computation.8 | async-start | bytes 1310720 | tf_op jit(solution)/shard_map/all_gather | solution.py:102
  11.3 401.2 %all-reduce.4.cloned.1.call-start = ((), (), s32[]{:S(2)}) async-start(), calls=%async_computation.9 | async-start | bytes 33554432 | tf_op jit(solution)/shard_map/psum | solution.py:138
  13.2 150.0 %copy-start.26 = (f32[512,64]{1,0:T(8,128)}, f32[512,64]{1,0:T(8,128)S(1)}, u32[]{:S(2)}) copy-start(f32[512,64]{1,0:T(8,128)S(1)} %get-tuple-element.124) | copy-start | bytes 393220
  160.7 8.2 copy-start.14
  184.8 9.7 copy-start.1
  194.5 323.5 %all-gather.14.cloned.1.call-start = ((), (), s32[]{:S(2)}) async-start(), calls=%async_computation.10 | async-start | bytes 7004160 | tf_op jit(solution)/shard_map/all_gather | solution.py:103
  198.4 377.9 %all-gather.16.cloned.1.call-start = ((), (), s32[]{:S(2)}) async-start(), calls=%async_computation.11 | async-start | bytes 3522560 | tf_op jit(solution)/shard_map/all_gather | solution.py:104
  200.7 511.8 %all-reduce.6.cloned.1.call-start = ((), (), s32[]{:S(2)}) async-start(), calls=%async_computation.12 | async-start | bytes 16777216 | tf_op jit(solution)/shard_map/psum | solution.py:148
  545.8 41.6 %copy-start.24 = (bf16[2048,684]{0,1:T(8,128)(2,1)}, bf16[2048,684]{0,1:T(8,128)(2,1)S(1)}, u32[]{:S(2)}) copy-start(bf16[2048,684]{0,1:T(8,128)(2,1)S(1)} %multiply_convert_fusion.2) | copy-start | bytes 8404996
  587.5 186.2 %all-gather.18.cloned.1.call-start = ((), (), s32[]{:S(2)}) async-start(), calls=%async_computation.13 | async-start | bytes 9437184 | tf_op jit(solution)/shard_map/all_gather | solution.py:155
  588.2 127.0 %copy-start.20 = (bf16[256,2048]{1,0:T(8,128)(2,1)S(1)}, bf16[256,2048]{1,0:T(8,128)(2,1)}, u32[]{:S(2)}) copy-start(bf16[256,2048]{1,0:T(8,128)(2,1)} %param.21) | copy-start | bytes 3145732
  719.1 162.0 %reduce-scatter.7.cloned.1.call-start = ((), (), s32[]{:S(2)}) async-start(), calls=%async_computation.14 | async-start | bytes 9437184 | tf_op jit(solution)/shard_map/reduce_scatter | solution.py:177
  809.5 133.2 %all-gather.20.cloned.1.call-start = ((), (), s32[]{:S(2)}) async-start(), calls=%async_computation.15 | async-start | bytes 9437184 | tf_op jit(solution)/shard_map/all_gather | solution.py:184
  888.3 181.1 %reduce-scatter.15.cloned.1.call-start = ((), (), s32[]{:S(2)}) async-start(), calls=%async_computation.19 | async-start | bytes 7045120 | tf_op jit(solution)/shard_map/reduce_scatter | solution.py:237
  907.0 196.4 %reduce-scatter.17.cloned.1.call-start = ((), (), s32[]{:S(2)}) async-start(), calls=%async_computation.20 | async-start | bytes 3522560 | tf_op jit(solution)/shard_map/reduce_scatter | solution.py:240
  919.4 23.3 %copy-start.30 = (bf16[256,2048]{1,0:T(8,128)(2,1)S(1)}, bf16[256,2048]{1,0:T(8,128)(2,1)}, u32[]{:S(2)}) copy-start(bf16[256,2048]{1,0:T(8,128)(2,1)} %all-gather.12.cloned.1.call-done) | copy-start | bytes 3145732
  919.5 213.3 %reduce-scatter.13.cloned.1.call-start = ((), (), s32[]{:S(2)}) async-start(), calls=%async_computation.18 | async-start | bytes 1310720 | tf_op jit(solution)/shard_map/reduce_scatter | solution.py:234
  984.3 6.9 copy-start.22
  991.1 202.7 %reduce-scatter.11.cloned.1.call-start = ((), (), s32[]{:S(2)}) async-start(), calls=%async_computation.17 | async-start | bytes 3932160 | tf_op jit(solution)/shard_map/reduce_scatter | solution.py:231
  1005.3 263.3 %reduce-scatter.9.cloned.1.call-start = ((), (), s32[]{:S(2)}) async-start(), calls=%async_computation.16 | async-start | bytes 9437184 | tf_op jit(solution)/shard_map/reduce_scatter | solution.py:225
  1019.4 5.4 copy-start.40
  1019.4 5.4 copy-start.41
  1021.0 48.5 %copy-start.4 = (f32[512,2,684]{0,1,2:T(2,128)S(1)}, f32[512,2,684]{0,1,2:T(2,128)}, u32[]{:S(2)}) copy-start(f32[512,2,684]{0,1,2:T(2,128)} %param.27) | copy-start | bytes 8404996
  1082.1 21.3 %copy-start.19 = (f32[684,512]{1,0:T(8,128)S(1)}, f32[684,512]{1,0:T(8,128)}, u32[]{:S(2)}) copy-start(f32[684,512]{1,0:T(8,128)} %param.28) | copy-start | bytes 4202500
  1082.1 21.3 %copy-start.29 = (f32[684,512]{1,0:T(8,128)S(1)}, f32[684,512]{1,0:T(8,128)}, u32[]{:S(2)}) copy-start(f32[684,512]{1,0:T(8,128)} %param.33) | copy-start | bytes 4202500
  1108.6 85.3 %copy-start.17 = (f32[512,3,256]{0,2,1:T(8,128)S(1)}, f32[512,3,256]{0,2,1:T(8,128)}, u32[]{:S(2)}) copy-start(f32[512,3,256]{0,2,1:T(8,128)} %copy.125) | copy-start | bytes 4718596
  1108.6 85.3 %copy-start.18 = (f32[512,3,256]{0,2,1:T(8,128)S(1)}, f32[512,3,256]{0,2,1:T(8,128)}, u32[]{:S(2)}) copy-start(f32[512,3,256]{0,2,1:T(8,128)} %copy.121) | copy-start | bytes 4718596
  1202.4 66.2 %copy-start.13 = (f32[256,2048]{1,0:T(8,128)S(1)}, f32[256,2048]{1,0:T(8,128)}, u32[]{:S(2)}) copy-start(f32[256,2048]{1,0:T(8,128)} %get-tuple-element.94) | copy-start | bytes 6291460
  (33 other events, 85.8 us)
Sparse Core Ops, SparseCore 0:
  10.2 66.1 all-gather.9
  78.3 52.8 all-gather.7
  133.3 27.9 all-gather.11
  194.6 217.7 all-reduce.3
  414.4 103.5 all-gather.13
  520.0 56.2 all-gather.15
  587.6 124.8 all-reduce.5
  719.3 54.3 all-gather.17
  809.6 71.4 reduce-scatter.6
  888.5 54.2 all-gather.19
  945.1 100.1 reduce-scatter.14
  1047.4 55.9 reduce-scatter.16
  1105.7 26.9 reduce-scatter.12
  1134.9 58.8 reduce-scatter.10
  1197.2 71.3 reduce-scatter.8
where the time goes:
time: 1290 us; the launch traced here: 1280 us
  waiting for transfers between devices  856 us (66%)
  matrix products  171 us (13%)
  other arithmetic  105 us (8%)
  local copies, waits for them, and re-layouts  89.7 us (7%)
  blocking collectives  41.6 us (3%)
  between operations  15 us (1%)
    psum x1, waiting for transfers between devices, local(): attn_total = lax.psum(attn_part, 'mp')  212 us
    psum x1, waiting for transfers between devices, local(): lax.psum(ffn_part.astype(jnp.bfloat16), 'mp').astype(jnp.float32)  124 us
    all_gather x1, waiting for transfers between devices, local(): lax.all_gather(gateup_weight.astype(jnp.bfloat16), 'dp', axis=0, tiled=True)  69.6 us
    reduce_scatter x1, waiting for transfers between devices, local(): lax.psum_scatter(middle_part.astype(jnp.bfloat16), 'mp', scatter_dimensio...  67.7 us
    all_gather x1, waiting for transfers between devices, local(): lax.all_gather(qkv_weight.astype(jnp.bfloat16), 'dp', axis=0, tiled=True)  61.7 us
    reduce_scatter x1, waiting for transfers between devices, local(): lax.psum_scatter(input_part.astype(jnp.bfloat16), 'mp', scatter_dimension...  59.7 us
    reduce_scatter x1, waiting for transfers between devices, local(): lax.psum_scatter(qkv_grad.astype(jnp.bfloat16), 'dp', scatter_dimension=0...  57.5 us
    all_gather x1, waiting for transfers between devices, local(): input_all = lax.all_gather(block_input, 'mp', axis=0, tiled=True)  54.8 us
  transfers between devices with their start and end apart: 15, of which 13 were waited for; matrix products, arithmetic and copies ran while one was open for 22% of the time, Pallas kernels for 0%

commit v1 on v0

--- a/solution.py
+++ b/solution.py
@@ -1,3 +1,4 @@
+import functools
 import jax
 import jax.numpy as jnp
 from jax import lax
@@ -16,6 +17,26 @@
 beta_two = 0.5
 adam_eps = 1e-08
 decay_rate = 0.1
+
+
+def _supply_panels(x_in, out_dim):
+    n = jax.lax.axis_size("mp")
+    seen = [(kk, (kk + 1) % n) for kk in range(n)]
+    line_up = [(kk, (kk - 1) % n) for kk in range(n)]
+    q_next, lower = ([x_in], [x_in])
+    for _ in range(n // 2):
+        q_next.append(jax.lax.ppermute(q_next[-1], axis_name="mp", perm=seen))
+    for _ in range((n - 1) // 2):
+        lower.append(jax.lax.ppermute(lower[-1], axis_name="mp", perm=line_up))
+    val = jnp.roll(
+        jnp.concatenate([*q_next[::-1], *lower[1:]], axis=out_dim),
+        shift=(jax.lax.axis_index("mp") - n // 2) * x_in.shape[out_dim],
+        axis=out_dim,
+    )
+    return val
+
+
+meet_indices = functools.partial(_supply_panels, out_dim=0)
 
 
 def rope_tables(seq_len, head_dim):
@@ -152,7 +173,7 @@
     mask_f32 = target_mask.astype(jnp.float32)
     grad_rows = out_cotangent.astype(jnp.float32) * mask_f32[:, None]
     grad_two, gain_two, bias_two = norm_backward(grad_rows, normed_two, inv_two, norm_params[2])
-    ffn_back = lax.all_gather(grad_two.astype(jnp.bfloat16), "mp", axis=0, tiled=True)
+    ffn_back = meet_indices(grad_two.astype(jnp.bfloat16))
     gate_again = jnp.einsum(
         "td,dcf->tcf", middle_low, gateup_full, preferred_element_type=jnp.float32
     )

time: 1290 us -> 1350 us (1.047)
  waiting for transfers between devices: 856 us -> 887 us
  local copies, waits for them, and re-layouts: 89.7 us -> 115 us
    ppermute x0 -> x7, waiting for transfers between devices: none -> 85.4 us  [the longest x4 85.4 us: _supply_panels(): q_next.append(jax.lax.ppermute(q_next[-1], axis_name='mp', perm=seen))]
    all_gather x1 -> x0, waiting for transfers between devices: 54.5 us -> none  [local(): lax.all_gather(grad_two.astype(jnp.bfloat16), 'mp', axis=0, tiled=True)]
    unnamed x112 -> x141, local copies, waits for them, and re-layouts: 47.2 us -> 71.2 us
  transfers between devices with their start and end apart: 15 -> 21, of which waited for: 13 -> 16; matrix products, arithmetic and copies ran while one was open for 22% -> 22% of each run, Pallas kernels for 0% -> 0%
where the time goes in v1:
time: 1350 us; the launch traced here: 1340 us
  waiting for transfers between devices  887 us (66%)
  matrix products  173 us (13%)
  local copies, waits for them, and re-layouts  115 us (9%)
  other arithmetic  104 us (8%)
  blocking collectives  41.4 us (3%)
  between operations  15.1 us (1%)
    psum x1, waiting for transfers between devices, local(): attn_total = lax.psum(attn_part, 'mp')  212 us
    psum x1, waiting for transfers between devices, local(): lax.psum(ffn_part.astype(jnp.bfloat16), 'mp').astype(jnp.float32)  124 us
    ppermute x4, waiting for transfers between devices, _supply_panels(): q_next.append(jax.lax.ppermute(q_next[-1], axis_name='mp', perm=seen))  85.4 us
    unnamed x141, local copies, waits for them, and re-layouts  71.2 us
    all_gather x1, waiting for transfers between devices, local(): lax.all_gather(gateup_weight.astype(jnp.bfloat16), 'dp', axis=0, tiled=True)  69.6 us
    reduce_scatter x1, waiting for transfers between devices, local(): lax.psum_scatter(middle_part.astype(jnp.bfloat16), 'mp', scatter_dimensio...  67.5 us
    all_gather x1, waiting for transfers between devices, local(): lax.all_gather(qkv_weight.astype(jnp.bfloat16), 'dp', axis=0, tiled=True)  61.7 us
    reduce_scatter x1, waiting for transfers between devices, local(): lax.psum_scatter(input_part.astype(jnp.bfloat16), 'mp', scatter_dimension...  59.7 us
  transfers between devices with their start and end apart: 21, of which 16 were waited for; matrix products, arithmetic and copies ran while one was open for 22% of the time, Pallas kernels for 0%

profile of v1, /device:TPU:0, one launch (start us, length us, event | category | flops | bytes accessed | tf_op | source)
XLA Modules:
  0.0 1344.0 jit_solution(15949026294555650534)
XLA Ops:
  14.7 61.7 %all-gather.9.cloned.1.call-done = bf16[2048,3,256]{2,0,1:T(8,128)(2,1)} async-done(((bf16[512,3,256]{2,0,1:T(8,128)(2,1)}), bf16[2048,3,256]{2,0,1:T(8,128)(2,1)}) %all-gather.9.cloned.1.call-update) | async-done | bytes 3145744 | tf_op jit(solution)/shard_map/all_gather | solution.py:122
  76.4 54.8 %all-gather.7.cloned.1.call-done = bf16[2048,2048]{1,0:T(8,128)(2,1)} async-done(((bf16[256,2048]{1,0:T(8,128)(2,1)}), bf16[2048,2048]{1,0:T(8,128)(2,1)}) %all-gather.7.cloned.1.call-update) | async-done | bytes 8388624 | tf_op jit(solution)/shard_map/all_gather | solution.py:127
  131.2 11.6 fusion.6
  142.8 8.3 reshape.239
  173.4 11.4 copy.105
  184.8 9.7 fusion.58
  200.9 211.6 %all-reduce.4.cloned.1.call-done = f32[2048,2048]{1,0:T(8,128)} async-done(((f32[2048,2048]{1,0:T(8,128)}), f32[2048,2048]{1,0:T(8,128)}) %all-reduce.4.cloned.1.call-update) | async-done | bytes 16777232 | tf_op jit(solution)/shard_map/psum | solution.py:159
  412.5 16.0 %fusion.90 = (f32[2048]{0:T(1024)S(1)}, f32[2048,2048]{1,0:T(8,128)}) fusion(f32[2048,2048]{1,0:T(8,128)} %all-reduce.4.cloned.1.call-done, bf16[2048,2048]{1,0:T(8,128)(2,1)} %all-gather.7.cloned.1.call-done), kind=kLoop, calls=%fused_computation.188 | loop fusion | flops 16775168 | bytes 41951232 | tf_op jit(solution)/shard_map/reduce_sum | solution.py:61
  428.5 7.7 multiply_reduce_fusion
  436.2 12.2 multiply_add_fusion
  448.5 69.6 %all-gather.13.cloned.1.call-done = bf16[2048,2,684]{0,1,2:T(2,128)(2,1)} async-done(((bf16[512,2,684]{0,1,2:T(2,128)(2,1)}), bf16[2048,2,684]{0,1,2:T(2,128)(2,1)}) %all-gather.13.cloned.1.call-update) | async-done | bytes 5603344 | tf_op jit(solution)/shard_map/all_gather | solution.py:124
  518.1 22.2 %fusion.2 = f32[2048,2,684]{0,2,1:T(8,128)} fusion(bf16[2048,2,684]{0,1,2:T(2,128)(2,1)} %all-gather.13.cloned.1.call-done, f32[2048,2048]{1,0:T(8,128)} %multiply_add_fusion), kind=kOutput, calls=%fused_computation.7 | convolution fusion | flops 11479810048 | bytes 33587200 | tf_op jit(solution)/shard_map/td,dcf->tcf/dot_general | solution.py:166
  545.9 30.5 %all-gather.15.cloned.1.call-done = bf16[684,2048]{1,0:T(8,128)(2,1)} async-done(((bf16[684,512]{1,0:T(8,128)(2,1)}), bf16[684,2048]{1,0:T(8,128)(2,1)}) %all-gather.15.cloned.1.call-update) | async-done | bytes 2801680 | tf_op jit(solution)/shard_map/all_gather | solution.py:125
  576.3 11.0 convolution_convert_fusion
  588.0 124.4 %all-reduce.6.cloned.1.call-done = bf16[2048,2048]{1,0:T(8,128)(2,1)} async-done(((bf16[2048,2048]{1,0:T(8,128)(2,1)}), bf16[2048,2048]{1,0:T(8,128)(2,1)}) %all-reduce.6.cloned.1.call-update) | async-done | bytes 8388624 | tf_op jit(solution)/shard_map/psum | solution.py:169
  718.6 15.1 %collective-permute-done = bf16[256,2048]{1,0:T(8,128)(2,1)S(1)} collective-permute-done((bf16[256,2048]{1,0:T(8,128)(2,1)S(1)}, bf16[256,2048]{1,0:T(8,128)(2,1)S(1)}, u32[]{:S(2)}, u32[]{:S(2)}) %collective-permute-start) | collective-permute-done | bytes 1048608 | tf_op jit(solution)/shard_map/ppermute | solution.py:28
  736.4 23.6 %collective-permute-done.1 = bf16[256,2048]{1,0:T(8,128)(2,1)S(1)} collective-permute-done((bf16[256,2048]{1,0:T(8,128)(2,1)S(1)}, bf16[256,2048]{1,0:T(8,128)(2,1)S(1)}, u32[]{:S(2)}, u32[]{:S(2)}) %collective-permute-start.1) | collective-permute-done | bytes 1048608 | tf_op jit(solution)/shard_map/ppermute | solution.py:28
  762.6 23.5 %collective-permute-done.2 = bf16[256,2048]{1,0:T(8,128)(2,1)} collective-permute-done((bf16[256,2048]{1,0:T(8,128)(2,1)S(1)}, bf16[256,2048]{1,0:T(8,128)(2,1)}, u32[]{:S(2)}, u32[]{:S(2)}) %collective-permute-start.2) | collective-permute-done | bytes 1048608 | tf_op jit(solution)/shard_map/ppermute | solution.py:28
  788.8 23.1 %collective-permute-done.3 = bf16[256,2048]{1,0:T(8,128)(2,1)} collective-permute-done((bf16[256,2048]{1,0:T(8,128)(2,1)}, bf16[256,2048]{1,0:T(8,128)(2,1)}, u32[]{:S(2)}, u32[]{:S(2)}) %collective-permute-start.3) | collective-permute-done | bytes 1048608 | tf_op jit(solution)/shard_map/ppermute | solution.py:28
  839.4 14.3 %fusion.43 = (bf16[2048,1,684]{0,2,1:T(8,128)(2,1)}, bf16[2048,1,684]{0,2,1:T(8,128)(2,1)}) fusion(f32[2048,2,684]{0,2,1:T(8,128)S(1)} %bitcast.110, f32[684]{0:T(1024)S(1)} %fusion.73, bf16[684,2048]{1,0:T(8,128)(2,1)S(1)} %copy-done.52, bf16[4096,2048]{1,0:T(8,128)(2,1)} %constant_dynamic-update-slice_fusion, s32[]{:T(128)S(6)} %select_n.26), kind=kOutput, calls=%fused_computation.60 | convolution fusion | flops 5772828672 | bytes 28002996 | tf_op jit(solution)/shard_map/td,fd->tf/dot_general | solution.py:184
  853.8 20.9 %bitcast_convert_fusion.1 = bf16[2048,2048]{1,0:T(8,128)(2,1)} fusion(bf16[2048,2,684]{0,1,2:T(2,128)(2,1)} %all-gather.13.cloned.1.call-done, bf16[2048,1,684]{0,2,1:T(8,128)(2,1)} %get-tuple-element.102, bf16[2048,1,684]{0,2,1:T(8,128)(2,1)} %get-tuple-element.101), kind=kOutput, calls=%fused_computation.1 | convolution fusion | flops 11482611712 | bytes 19595264 | tf_op jit(solution)/shard_map/tcf,dcf->td/dot_general | solution.py:191
  878.7 67.5 %reduce-scatter.7.cloned.1.call-done = bf16[256,2048]{1,0:T(8,128)(2,1)} async-done(((bf16[2048,2048]{1,0:T(8,128)(2,1)}), bf16[256,2048]{1,0:T(8,128)(2,1)}) %reduce-scatter.7.cloned.1.call-update) | async-done | bytes 1048592 | tf_op jit(solution)/shard_map/reduce_scatter | solution.py:198
  953.5 18.7 %fusion.23 = bf16[2048,2,684]{0,2,1:T(8,128)(2,1)} fusion(f32[2048,2048]{1,0:T(8,128)} %multiply_add_fusion, bf16[2048,1,684]{0,2,1:T(8,128)(2,1)} %get-tuple-element.102, bf16[2048,1,684]{0,2,1:T(8,128)(2,1)} %get-tuple-element.101), kind=kOutput, calls=%fused_computation.43 | convolution fusion | flops 11493818368 | bytes 27983872 | tf_op jit(solution)/shard_map/td,tcf->dcf/dot_general | solution.py:194
  973.9 10.6 fusion.35
  985.3 22.5 %all-gather.17.cloned.1.call-done = bf16[2048,2048]{1,0:T(8,128)(2,1)} async-done(((bf16[256,2048]{1,0:T(8,128)(2,1)}), bf16[2048,2048]{1,0:T(8,128)(2,1)}) %all-gather.17.cloned.1.call-update) | async-done | bytes 8388624 | tf_op jit(solution)/shard_map/all_gather | solution.py:205
  1058.4 12.0 fusion.38
  1072.3 10.8 bitcast_convert_fusion
  1093.0 41.4 %all-reduce = (f32[]{:T(128)}, f32[4,2048]{1,0:T(4,128)S(1)}) all-reduce(f32[]{:T(128)} %convert_reduce_fusion, f32[4,2048]{1,0:T(4,128)S(1)} %pad_maximum_fusion.11), channel_id=1, replica_groups=mesh['dp'=4,'mp'=8] {'dp','mp'}, use_global_device_ids=true, to_apply=%region_18.19 | all-reduce | flops 8193 | bytes 65544 | tf_op jit(solution)/shard_map/psum | solution.py:266
  1152.1 16.4 %reduce-scatter.17.cloned.1.call-done = bf16[684,512]{1,0:T(8,128)(2,1)} async-done(((bf16[684,2048]{1,0:T(8,128)(2,1)}), bf16[684,512]{1,0:T(8,128)(2,1)}) %reduce-scatter.17.cloned.1.call-update) | async-done | bytes 700432 | tf_op jit(solution)/shard_map/reduce_scatter | solution.py:261
  1173.5 24.1 %reduce-scatter.13.cloned.1.call-done = bf16[256,512]{1,0:T(8,128)(2,1)} async-done(((bf16[256,2048]{1,0:T(8,128)(2,1)}), bf16[256,512]{1,0:T(8,128)(2,1)}) %reduce-scatter.13.cloned.1.call-update) | async-done | bytes 262160 | tf_op jit(solution)/shard_map/reduce_scatter | solution.py:255
  1201.1 57.7 %reduce-scatter.11.cloned.1.call-done = bf16[512,3,256]{0,2,1:T(8,128)(2,1)} async-done(((bf16[2048,3,256]{0,2,1:T(8,128)(2,1)}), bf16[512,3,256]{0,2,1:T(8,128)(2,1)}) %reduce-scatter.11.cloned.1.call-update) | async-done | bytes 786448 | tf_op jit(solution)/shard_map/reduce_scatter | solution.py:252
  1273.9 59.7 %reduce-scatter.9.cloned.1.call-done = bf16[256,2048]{1,0:T(8,128)(2,1)} async-done(((bf16[2048,2048]{1,0:T(8,128)(2,1)}), bf16[256,2048]{1,0:T(8,128)(2,1)}) %reduce-scatter.9.cloned.1.call-update) | async-done | bytes 1048592 | tf_op jit(solution)/shard_map/reduce_scatter | solution.py:246
  (250 shorter events, 204.1 us)
Async XLA Ops:
  7.2 69.1 %all-gather.9.cloned.1.call-start = ((), (), s32[]{:S(2)}) async-start(), calls=%async_computation.7 | async-start | bytes 3932160 | tf_op jit(solution)/shard_map/all_gather | solution.py:122
  9.7 121.5 %all-gather.7.cloned.1.call-start = ((), (), s32[]{:S(2)}) async-start(), calls=%async_computation.6 | async-start | bytes 9437184 | tf_op jit(solution)/shard_map/all_gather | solution.py:127
  10.5 174.4 %all-gather.11.cloned.1.call-start = ((), (), s32[]{:S(2)}) async-start(), calls=%async_computation.8 | async-start | bytes 1310720 | tf_op jit(solution)/shard_map/all_gather | solution.py:123
  11.3 401.2 %all-reduce.4.cloned.1.call-start = ((), (), s32[]{:S(2)}) async-start(), calls=%async_computation.9 | async-start | bytes 33554432 | tf_op jit(solution)/shard_map/psum | solution.py:159
  13.2 150.0 %copy-start.31 = (f32[512,64]{1,0:T(8,128)}, f32[512,64]{1,0:T(8,128)S(1)}, u32[]{:S(2)}) copy-start(f32[512,64]{1,0:T(8,128)S(1)} %get-tuple-element.124) | copy-start | bytes 393220
  194.6 323.5 %all-gather.13.cloned.1.call-start = ((), (), s32[]{:S(2)}) async-start(), calls=%async_computation.10 | async-start | bytes 7004160 | tf_op jit(solution)/shard_map/all_gather | solution.py:124
  198.4 377.9 %all-gather.15.cloned.1.call-start = ((), (), s32[]{:S(2)}) async-start(), calls=%async_computation.11 | async-start | bytes 3522560 | tf_op jit(solution)/shard_map/all_gather | solution.py:125
  200.8 511.6 %all-reduce.6.cloned.1.call-start = ((), (), s32[]{:S(2)}) async-start(), calls=%async_computation.12 | async-start | bytes 16777216 | tf_op jit(solution)/shard_map/psum | solution.py:169
  545.8 41.4 %copy-start.29 = (bf16[2048,684]{0,1:T(8,128)(2,1)}, bf16[2048,684]{0,1:T(8,128)(2,1)S(1)}, u32[]{:S(2)}) copy-start(bf16[2048,684]{0,1:T(8,128)(2,1)S(1)} %multiply_convert_fusion.2) | copy-start | bytes 8404996
  587.3 358.9 %reduce-scatter.7.cloned.1.call-start = ((), (), s32[]{:S(2)}) async-start(), calls=%async_computation.13 | async-start | bytes 9437184 | tf_op jit(solution)/shard_map/reduce_scatter | solution.py:198
  588.0 127.0 %copy-start.20 = (bf16[256,2048]{1,0:T(8,128)(2,1)S(1)}, bf16[256,2048]{1,0:T(8,128)(2,1)}, u32[]{:S(2)}) copy-start(bf16[256,2048]{1,0:T(8,128)(2,1)} %param.21) | copy-start | bytes 3145732
  718.6 15.1 %collective-permute-start = (bf16[256,2048]{1,0:T(8,128)(2,1)S(1)}, bf16[256,2048]{1,0:T(8,128)(2,1)S(1)}, u32[]{:S(2)}, u32[]{:S(2)}) collective-permute-start(bf16[256,2048]{1,0:T(8,128)(2,1)S(1)} %get-tuple-element.95), channel_id=1, source_target_pairs={{0,1},{1,2},{2,3},{3,4},{4,5},{5,6},{6,7},{7,0},{8,9},{9,10},{10,1... | collective-permute-start | bytes 3145736 | tf_op jit(solution)/shard_map/ppermute | solution.py:28
  733.7 26.3 %copy-start.22 = (bf16[256,2048]{1,0:T(8,128)(2,1)}, bf16[256,2048]{1,0:T(8,128)(2,1)S(1)}, u32[]{:S(2)}) copy-start(bf16[256,2048]{1,0:T(8,128)(2,1)S(1)} %collective-permute-done) | copy-start | bytes 3145732
  733.7 26.3 %collective-permute-start.1 = (bf16[256,2048]{1,0:T(8,128)(2,1)S(1)}, bf16[256,2048]{1,0:T(8,128)(2,1)S(1)}, u32[]{:S(2)}, u32[]{:S(2)}) collective-permute-start(bf16[256,2048]{1,0:T(8,128)(2,1)S(1)} %collective-permute-done), channel_id=1, source_target_pairs={{0,1},{1,2},{2,3},{3,4},{4,5},{5,6},{6,7},{7,0},{8,9},{9,10},{10,1... | collective-permute-start | bytes 3145736 | tf_op jit(solution)/shard_map/ppermute | solution.py:28
  733.7 26.3 %collective-permute-start.4 = (bf16[256,2048]{1,0:T(8,128)(2,1)S(1)}, bf16[256,2048]{1,0:T(8,128)(2,1)}, u32[]{:S(2)}, u32[]{:S(2)}) collective-permute-start(bf16[256,2048]{1,0:T(8,128)(2,1)S(1)} %get-tuple-element.95), channel_id=1, source_target_pairs={{0,7},{1,0},{2,1},{3,2},{4,3},{5,4},{6,5},{7,6},{8,15},{9,8},{10,9... | collective-permute-start | bytes 3145736 | tf_op jit(solution)/shard_map/ppermute | solution.py:30
  760.0 26.2 %collective-permute-start.2 = (bf16[256,2048]{1,0:T(8,128)(2,1)S(1)}, bf16[256,2048]{1,0:T(8,128)(2,1)}, u32[]{:S(2)}, u32[]{:S(2)}) collective-permute-start(bf16[256,2048]{1,0:T(8,128)(2,1)S(1)} %collective-permute-done.1), channel_id=1, source_target_pairs={{0,1},{1,2},{2,3},{3,4},{4,5},{5,6},{6,7},{7,0},{8,9},{9,10},{10,1... | collective-permute-start | bytes 3145736 | tf_op jit(solution)/shard_map/ppermute | solution.py:28
  760.0 26.2 %collective-permute-start.5 = (bf16[256,2048]{1,0:T(8,128)(2,1)}, bf16[256,2048]{1,0:T(8,128)(2,1)}, u32[]{:S(2)}, u32[]{:S(2)}) collective-permute-start(bf16[256,2048]{1,0:T(8,128)(2,1)} %collective-permute-done.4), channel_id=1, source_target_pairs={{0,7},{1,0},{2,1},{3,2},{4,3},{5,4},{6,5},{7,6},{8,15},{9,8},{10,9... | collective-permute-start | bytes 3145736 | tf_op jit(solution)/shard_map/ppermute | solution.py:30
  786.2 25.8 %collective-permute-start.3 = (bf16[256,2048]{1,0:T(8,128)(2,1)}, bf16[256,2048]{1,0:T(8,128)(2,1)}, u32[]{:S(2)}, u32[]{:S(2)}) collective-permute-start(bf16[256,2048]{1,0:T(8,128)(2,1)} %collective-permute-done.2), channel_id=1, source_target_pairs={{0,1},{1,2},{2,3},{3,4},{4,5},{5,6},{6,7},{7,0},{8,9},{9,10},{10,1... | collective-permute-start | bytes 3145736 | tf_op jit(solution)/shard_map/ppermute | solution.py:28
  786.2 30.4 %copy-start.25 = (bf16[256,2048]{1,0:T(8,128)(2,1)S(1)}, bf16[256,2048]{1,0:T(8,128)(2,1)}, u32[]{:S(2)}) copy-start(bf16[256,2048]{1,0:T(8,128)(2,1)} %copy-done.24) | copy-start | bytes 3145732
  786.2 31.4 %copy-start.23 = (bf16[256,2048]{1,0:T(8,128)(2,1)S(1)}, bf16[256,2048]{1,0:T(8,128)(2,1)}, u32[]{:S(2)}) copy-start(bf16[256,2048]{1,0:T(8,128)(2,1)} %copy-done.22) | copy-start | bytes 3145732
  786.2 38.3 %collective-permute-start.6 = (bf16[256,2048]{1,0:T(8,128)(2,1)}, bf16[256,2048]{1,0:T(8,128)(2,1)S(1)}, u32[]{:S(2)}, u32[]{:S(2)}) collective-permute-start(bf16[256,2048]{1,0:T(8,128)(2,1)} %collective-permute-done.5), channel_id=1, source_target_pairs={{0,7},{1,0},{2,1},{3,2},{4,3},{5,4},{6,5},{7,6},{8,15},{9,8},{10,9... | collective-permute-start | bytes 3145736 | tf_op jit(solution)/shard_map/ppermute | solution.py:30
  874.7 133.1 %all-gather.17.cloned.1.call-start = ((), (), s32[]{:S(2)}) async-start(), calls=%async_computation.14 | async-start | bytes 9437184 | tf_op jit(solution)/shard_map/all_gather | solution.py:205
  953.4 181.0 %reduce-scatter.15.cloned.1.call-start = ((), (), s32[]{:S(2)}) async-start(), calls=%async_computation.18 | async-start | bytes 7045120 | tf_op jit(solution)/shard_map/reduce_scatter | solution.py:258
  972.2 196.3 %reduce-scatter.17.cloned.1.call-start = ((), (), s32[]{:S(2)}) async-start(), calls=%async_computation.19 | async-start | bytes 3522560 | tf_op jit(solution)/shard_map/reduce_scatter | solution.py:261
  984.6 23.3 %copy-start.35 = (bf16[256,2048]{1,0:T(8,128)(2,1)S(1)}, bf16[256,2048]{1,0:T(8,128)(2,1)}, u32[]{:S(2)}) copy-start(bf16[256,2048]{1,0:T(8,128)(2,1)} %all-gather.11.cloned.1.call-done) | copy-start | bytes 3145732
  984.6 213.0 %reduce-scatter.13.cloned.1.call-start = ((), (), s32[]{:S(2)}) async-start(), calls=%async_computation.17 | async-start | bytes 1310720 | tf_op jit(solution)/shard_map/reduce_scatter | solution.py:255
  1056.3 202.6 %reduce-scatter.11.cloned.1.call-start = ((), (), s32[]{:S(2)}) async-start(), calls=%async_computation.16 | async-start | bytes 3932160 | tf_op jit(solution)/shard_map/reduce_scatter | solution.py:252
  1070.4 263.2 %reduce-scatter.9.cloned.1.call-start = ((), (), s32[]{:S(2)}) async-start(), calls=%async_computation.15 | async-start | bytes 9437184 | tf_op jit(solution)/shard_map/reduce_scatter | solution.py:246
  1086.1 48.2 %copy-start.4 = (f32[512,2,684]{0,1,2:T(2,128)S(1)}, f32[512,2,684]{0,1,2:T(2,128)}, u32[]{:S(2)}) copy-start(f32[512,2,684]{0,1,2:T(2,128)} %param.27) | copy-start | bytes 8404996
  1173.5 85.3 %copy-start.17 = (f32[512,3,256]{0,2,1:T(8,128)S(1)}, f32[512,3,256]{0,2,1:T(8,128)}, u32[]{:S(2)}) copy-start(f32[512,3,256]{0,2,1:T(8,128)} %copy.125) | copy-start | bytes 4718596
  1173.5 85.3 %copy-start.18 = (f32[512,3,256]{0,2,1:T(8,128)S(1)}, f32[512,3,256]{0,2,1:T(8,128)}, u32[]{:S(2)}) copy-start(f32[512,3,256]{0,2,1:T(8,128)} %copy.121) | copy-start | bytes 4718596
  1267.3 66.3 %copy-start.13 = (f32[256,2048]{1,0:T(8,128)S(1)}, f32[256,2048]{1,0:T(8,128)}, u32[]{:S(2)}) copy-start(f32[256,2048]{1,0:T(8,128)} %get-tuple-element.94) | copy-start | bytes 6291460
  (46 other events, 223.2 us)
Sparse Core Ops, SparseCore 0:
  10.2 66.1 all-gather.8
  78.3 52.8 all-gather.6
  133.3 27.9 all-gather.10
  194.7 217.7 all-reduce.3
  414.5 103.5 all-gather.12
  520.1 56.2 all-gather.14
  587.4 124.8 all-reduce.5
  874.8 71.3 reduce-scatter.6
  953.5 54.2 all-gather.16
  1010.0 100.1 reduce-scatter.14
  1112.5 55.8 reduce-scatter.16
  1170.6 26.9 reduce-scatter.12
  1199.9 58.9 reduce-scatter.10
  1262.2 71.4 reduce-scatter.8
